TPU v7x, 512 devices: a whole 4x4x16 slice. The times are simulated.
512 devices in a mesh: clip: 4 (over y), frame: 8 (over x, z_hi), pix: 16 (over z_lo, core).
Axes of the slice: x: 4, y: 4, z: 16 (z_hi: 2, z_lo: 8; z = z_hi * 8 + z_lo), core: 2. Of those that a mesh axis runs over, the one named last changes fastest.
Arguments:
- features: bfloat16 [32, 32, 96, 256], P(('clip', 'frame'), 'pix'), parts along dimension 0, may hold values from -6 to 6
Outputs:
- forward_full: bfloat16 [32, 32, 96, 3072], P(('clip', 'frame'), 'pix'), parts along dimension 0
- forward_half: bfloat16 [32, 32, 96, 768], P(('clip', 'frame'), 'pix'), parts along dimension 0
- forward_quarter: bfloat16 [32, 32, 96, 192], P(('clip', 'frame'), 'pix'), parts along dimension 0
- forward_eighth: bfloat16 [32, 32, 96, 48], P(('clip', 'frame'), 'pix'), parts along dimension 0
- backward_full: bfloat16 [32, 32, 96, 3072], P(('clip', 'frame'), 'pix'), parts along dimension 0
- backward_half: bfloat16 [32, 32, 96, 768], P(('clip', 'frame'), 'pix'), parts along dimension 0
- backward_quarter: bfloat16 [32, 32, 96, 192], P(('clip', 'frame'), 'pix'), parts along dimension 0
- backward_eighth: bfloat16 [32, 32, 96, 48], P(('clip', 'frame'), 'pix'), parts along dimension 0
There are 4 independent parts, one for each index of `clip`. A program takes and returns all parts, laid end to end along the dimension named above; each array names one. Nothing has to cross between parts.
All inputs are finite; a program needn't handle non-finite values.
Results may differ from a plain program's by a relative error of at most 0.001.
Values may be sent and summed in bfloat16 or wider, within the bound.
A program may use at most 64 MiB of HBM per device.

v0:
```python
import math

import jax
import jax.numpy as jnp
from jax import lax
from jax.sharding import Mesh
from jax.sharding import PartitionSpec as P

PIX = ("pix_0", "pix_1")


def from_behind(value, axis, steps):
    count = lax.axis_size(axis)
    leading, last = (max(0, -steps), min(count, count - steps))
    return lax.ppermute(value, axis, [(source, source + steps) for source in range(leading, last)])


def sent_to_all(array, axis):
    devices = lax.axis_size(axis)
    return lax.all_to_all(
        jnp.broadcast_to(array[None], (devices, *array.shape)), axis, 0, 0, tiled=True
    )


def laid_out(blocks, dim):
    lengths = list(blocks.shape[1:])
    lengths[dim] *= blocks.shape[0]
    return jnp.moveaxis(blocks, 0, dim).reshape(lengths)


def gather_axes(array, axes, dim):
    far, near = axes
    blocks = sent_to_all(sent_to_all(array, far), near)
    return laid_out(blocks.swapaxes(0, 1).reshape(-1, *array.shape), dim)


def halved(current):
    count, height, breadth = current.shape
    return current.reshape(count, height // 2, 2, breadth // 2, 2).mean(axis=(2, 4))


def pyramid_of(scores, row_count, breadth):
    height = scores.shape[1] // breadth
    current = scores.reshape(scores.shape[0], height, breadth)
    result = []
    for depth_index in range(4):
        result.append(current.reshape(1, row_count, breadth, -1).astype(jnp.bfloat16))
        if depth_index < 3:
            current = halved(current)
    return result


def per_device(features):
    row_count = features.shape[1]
    breadth = features.shape[2]
    channels = features.shape[3]
    own_pixels = features.reshape(row_count * breadth, channels)
    factor = 1.0 / math.sqrt(channels)

    def against(target):
        product = lax.dot_general(
            own_pixels, target, (((1,), (1,)), ((), ())), preferred_element_type=jnp.float32
        )
        return product * factor

    later_pixels = from_behind(own_pixels, "frame", -1)
    earlier_pixels = from_behind(own_pixels, "frame", 1)
    paired = jnp.concatenate([later_pixels, earlier_pixels], axis=1)
    target = gather_axes(paired, ("pix_0", "pix_1"), 0)
    ahead = against(target[:, :channels])
    behind = against(target[:, channels:])
    stacked = jnp.stack([ahead, behind])
    forward = stacked[0]
    backward = stacked[1]
    forward_levels = pyramid_of(forward, row_count, breadth)
    backward_levels = pyramid_of(backward, row_count, breadth)
    return (
        forward_levels[0],
        forward_levels[1],
        forward_levels[2],
        forward_levels[3],
        backward_levels[0],
        backward_levels[1],
        backward_levels[2],
        backward_levels[3],
    )


def solution(mesh):
    finer = Mesh(
        mesh.devices.reshape(mesh.shape["clip"], mesh.shape["frame"], 8, 2),
        ("clip", "frame", "pix_0", "pix_1"),
    )
    in_specs = (P(("clip", "frame"), PIX, None, None),)
    out_specs = (
        P(("clip", "frame"), PIX, None, None),
        P(("clip", "frame"), PIX, None, None),
        P(("clip", "frame"), PIX, None, None),
        P(("clip", "frame"), PIX, None, None),
        P(("clip", "frame"), PIX, None, None),
        P(("clip", "frame"), PIX, None, None),
        P(("clip", "frame"), PIX, None, None),
        P(("clip", "frame"), PIX, None, None),
    )
    return jax.shard_map(
        per_device, mesh=finer, in_specs=in_specs, out_specs=out_specs, check_vma=False
    )
```

profile of v0, /device:TPU:1, one launch (start us, length us, event | category | flops | bytes accessed | tf_op | source)
XLA Modules:
  0.0 159.3 jit_solution(18370796622724767579)
XLA Ops:
  0.6 16.3 %collective-permute-start.1 = (bf16[192,256]{1,0:T(8,128)(2,1)}, bf16[192,256]{1,0:T(8,128)(2,1)S(1)}, u32[]{:S(2)}, u32[]{:S(2)}) collective-permute-start(bf16[192,256]{1,0:T(8,128)(2,1)} %bitcast.40), channel_id=1, source_target_pairs={{0,16},{16,32},{32,48},{48,64},{64,80},{80,96},{96,112},{1,17},{17... | collective-permute-start | bytes 294920 | tf_op jit(solution)/shard_map/ppermute | solution.py:15
  16.9 1.3 collective-permute-start
  18.2 0.7 collective-permute-done.1
  18.9 15.6 %collective-permute-done = bf16[192,256]{1,0:T(8,128)(2,1)S(1)} collective-permute-done((bf16[192,256]{1,0:T(8,128)(2,1)}, bf16[192,256]{1,0:T(8,128)(2,1)S(1)}, u32[]{:S(2)}, u32[]{:S(2)}) %collective-permute-start) | collective-permute-done | bytes 98336 | tf_op jit(solution)/shard_map/ppermute | solution.py:15
  34.7 78.3 %all_to_all.10 = bf16[8,192,512]{2,1,0:T(8,128)(2,1)S(1)} all-to-all(bf16[8,192,512]{2,1,0:T(8,128)(2,1)S(1)} %broadcast_in_dim.4), channel_id=1, replica_groups=mesh['clip'=4,'frame'=8,'pix_0'=8,'pix_1'=2] {'pix_0'}, dimensions={0} | all-to-all | bytes 3145728 | tf_op jit(solution)/shard_map/all_to_all | solution.py:20
  113.4 7.7 %all_to_all.11 = bf16[2,8,192,512]{3,2,1,0:T(8,128)(2,1)S(1)} all-to-all(bf16[2,8,192,512]{3,2,1,0:T(8,128)(2,1)S(1)} %broadcast_in_dim.5), channel_id=1, replica_groups=mesh['clip'=4,'frame'=8,'pix_0'=8,'pix_1'=2] {'pix_1'}, dimensions={0} | all-to-all | bytes 6291456 | tf_op jit(solution)/shard_map/all_to_all | solution.py:20
  121.4 0.6 copy-done.1
  122.0 1.7 %fusion.8 = (bf16[192,3072]{1,0:T(8,128)(2,1)}, f32[192,3072]{1,0:T(8,128)S(1)}) fusion(bf16[192,256]{1,0:T(8,128)(2,1)S(1)} %bitcast.42, bf16[3072,512]{1,0:T(8,128)(2,1)S(1)} %bitcast.36), kind=kOutput, calls=%fused_computation.17 | convolution fusion | flops 303169536 | bytes 5210112 | tf_op jit(solution)/shard_map/dot_general | solution.py:61
  123.7 2.5 %fusion.9 = (bf16[192,3072]{1,0:T(8,128)(2,1)}, f32[192,3072]{1,0:T(8,128)}) fusion(bf16[192,256]{1,0:T(8,128)(2,1)S(1)} %bitcast.43, bf16[3072,512]{1,0:T(8,128)(2,1)S(1)} %bitcast.37), kind=kOutput, calls=%fused_computation.18 | convolution fusion | flops 303169536 | bytes 5210112 | tf_op jit(solution)/shard_map/dot_general | solution.py:61
  126.2 2.3 %copy.18 = f32[192,3072]{0,1:T(8,128)} copy(f32[192,3072]{1,0:T(8,128)S(1)} %get-tuple-element.33) | data formatting | bytes 4718592 | tf_op jit(solution)/shard_map/mul | solution.py:64
  128.5 3.7 %reshape_reshape_squeeze_stack.8 = f32[192,16,2,48,2]{0,4,3,2,1:T(2,128)S(1)} reshape(f32[192,3072]{0,1:T(8,128)} %copy.18) | data formatting | bytes 4718592 | tf_op jit(solution)/shard_map/reshape;reshape;squeeze;stack | solution.py:39
  132.2 4.0 %reduce_sum.54 = f32[192,16,48]{0,2,1:T(8,128)} reduce(f32[192,16,2,48,2]{0,4,3,2,1:T(2,128)S(1)} %reshape_reshape_squeeze_stack.8, f32[]{:T(128)} %constant.12.clone.1), dimensions={2,4}, to_apply=%region_0.0 | reduce | flops 442368 | bytes 2949124 | tf_op jit(solution)/shard_map/reduce_sum | solution.py:39
  136.2 2.1 %broadcast_multiply_fusion.1 = (f32[192,16,48]{0,2,1:T(8,128)}, bf16[192,16,48]{0,2,1:T(8,128)(2,1)S(1)}) fusion(f32[192,16,48]{0,2,1:T(8,128)} %reduce_sum.54), kind=kLoop, calls=%fused_computation.7 | loop fusion | flops 294912 | bytes 1474560 | tf_op jit(solution)/shard_map/div | solution.py:39
  138.5 1.0 copy.20
  139.5 1.6 %div.27 = f32[192,8,2,24,2]{0,4,3,2,1:T(2,128)S(1)} reshape(f32[192,16,48]{0,2,1:T(8,128)} %get-tuple-element.26) | data formatting | bytes 1179648 | tf_op jit(solution)/shard_map/div | solution.py:39
  141.9 0.7 copy.21
  143.0 0.6 copy.22
  143.6 2.3 %copy.19 = f32[192,3072]{0,1:T(8,128)} copy(f32[192,3072]{1,0:T(8,128)S(1)} %copy-done) | data formatting | bytes 4718592 | tf_op jit(solution)/shard_map/mul | solution.py:64
  146.0 3.9 %reshape_reshape_squeeze_stack.9 = f32[192,16,2,48,2]{0,4,3,2,1:T(2,128)S(1)} reshape(f32[192,3072]{0,1:T(8,128)} %copy.19) | data formatting | bytes 4718592 | tf_op jit(solution)/shard_map/reshape;reshape;squeeze;stack | solution.py:39
  149.9 4.0 %reduce_sum.57 = f32[192,16,48]{0,2,1:T(8,128)} reduce(f32[192,16,2,48,2]{0,4,3,2,1:T(2,128)S(1)} %reshape_reshape_squeeze_stack.9, f32[]{:T(128)} %constant.12.clone.1), dimensions={2,4}, to_apply=%region_3.0 | reduce | flops 442368 | bytes 2949124 | tf_op jit(solution)/shard_map/reduce_sum | solution.py:39
  153.8 1.2 broadcast_multiply_fusion
  155.3 1.0 copy.23
  157.6 0.7 copy.24
  158.7 0.6 copy.25
  (24 shorter events, 3.9 us)
Async XLA Ops:
  0.6 18.3 %collective-permute-start.1 = (bf16[192,256]{1,0:T(8,128)(2,1)}, bf16[192,256]{1,0:T(8,128)(2,1)S(1)}, u32[]{:S(2)}, u32[]{:S(2)}) collective-permute-start(bf16[192,256]{1,0:T(8,128)(2,1)} %bitcast.40), channel_id=1, source_target_pairs={{0,16},{16,32},{32,48},{48,64},{64,80},{80,96},{96,112},{1,17},{17... | collective-permute-start | bytes 294920 | tf_op jit(solution)/shard_map/ppermute | solution.py:15
  16.9 17.6 %collective-permute-start = (bf16[192,256]{1,0:T(8,128)(2,1)}, bf16[192,256]{1,0:T(8,128)(2,1)S(1)}, u32[]{:S(2)}, u32[]{:S(2)}) collective-permute-start(bf16[192,256]{1,0:T(8,128)(2,1)} %bitcast.41), channel_id=1, source_target_pairs={{16,0},{32,16},{48,32},{64,48},{80,64},{96,80},{112,96},{17,1},{33... | collective-permute-start | bytes 294920 | tf_op jit(solution)/shard_map/ppermute | solution.py:15
  121.1 0.9 copy-start.1
  138.5 5.1 %copy-start = (f32[192,3072]{1,0:T(8,128)S(1)}, f32[192,3072]{1,0:T(8,128)}, u32[]{:S(2)}) copy-start(f32[192,3072]{1,0:T(8,128)} %get-tuple-element.35) | copy-start | bytes 7077892
where the time goes:
time: 161 us; the launch traced here: 159 us
  blocking collectives  86.1 us (53%)
  local copies, waits for them, and re-layouts  21.5 us (13%)
  starting transfers between devices  17.6 us (11%)
  waiting for transfers between devices  16.3 us (10%)
  other arithmetic  12.9 us (8%)
  matrix products  4.15 us (3%)
    all_to_all x2, blocking collectives, sent_to_all(): lax.all_to_all(jnp.broadcast_to(array[None], (devices, *array.shape)), ax...  86.1 us
    ppermute x2, starting transfers between devices, from_behind(): lax.ppermute(value, axis, [(source, source + steps) for source in range(l...  17.6 us
    ppermute x2, waiting for transfers between devices, from_behind(): lax.ppermute(value, axis, [(source, source + steps) for source in range(l...  16.3 us
    reduce_sum x6, other arithmetic, halved(): current.reshape(count, height // 2, 2, breadth // 2, 2).mean(axis=(2, 4))  9.43 us
    another operation x2, local copies, waits for them, and re-layouts, halved(): current.reshape(count, height // 2, 2, breadth // 2, 2).mean(axis=(2, 4))  7.65 us
    unnamed x10, local copies, waits for them, and re-layouts  5.38 us
    mul x2, local copies, waits for them, and re-layouts, against(): return product * factor  4.62 us
    dot_general x2, matrix products, against(): lax.dot_general(own_pixels, target, (((1,), (1,)), ((), ())), preferred_e...  4.15 us
  transfers between devices with their start and end apart: 2, of which 2 were waited for; matrix products, arithmetic and copies ran while one was open for 0% of the time, Pallas kernels for 0%

commit v1 on v0

v1 whole, which is shorter than its diff:
```python
import functools
import math

import jax
import jax.numpy as jnp
from jax import lax
from jax.experimental import pallas as pl
from jax.experimental.pallas import tpu as pltpu
from jax.sharding import PartitionSpec as P

MESH = pl.DeviceIdType.MESH
HOP = 2
SIDE = 2


def gather_kernel(frames, line, own, t, init_send, chain_send, x_send, p_send, chain_recv, x_recv, p_recv):
    half = own.shape[0] // 2
    reach = line // 2
    chunks = 2 * reach
    f = lax.axis_index("frame")
    p = lax.axis_index("pix")
    l = p // 2
    c = p % 2
    odd = f % 2
    sign = 1 - 2 * odd
    mate = f + sign
    other = (f - sign + frames) % frames
    ahead = (f + 2 * sign + frames) % frames
    behind = (f - 2 * sign + frames) % frames

    def at(frame, chip, core):
        return {"frame": frame, "pix": 2 * chip + core}

    barrier = pltpu.get_barrier_semaphore()

    def greet(frame, chip, core):
        pl.semaphore_signal(barrier, inc=1, device_id=at(frame, chip, core), device_id_type=MESH)

    greet(f, l, 1 - c)
    greet(ahead, l, c)
    greet(behind, l, c)

    @pl.when(l < line - 1)
    def _():
        greet(f, l + 1, c)

    @pl.when(l > 0)
    def _():
        greet(f, l - 1, c)

    @pl.when(l == line - 1)
    def _():
        for r in range(reach):
            greet(mate, r, c)
            greet(other, r, c)

    @pl.when(l == 0)
    def _():
        for r in range(reach):
            greet(mate, line - 1 - r, c)
            greet(other, line - 1 - r, c)

    inner = jnp.where((l > 0) & (l < line - 1), 1, 0)
    pl.semaphore_wait(barrier, 6 + inner)

    def place(slot, d, r, kind, core):
        source = jnp.where(d == 0, r, line - 1 - r)
        return t.at[slot, 2 * source + core, pl.ds(pl.multiple_of(kind * half, half), half)]

    my_d = jnp.where(l < reach, 0, 1)
    my_r = jnp.where(l < reach, l, line - 1 - l)
    entry = jnp.where(l < reach, line - 1, 0)

    def first(kind):
        return pltpu.make_async_remote_copy(
            src_ref=own.at[pl.ds(kind * half, half)],
            dst_ref=place(odd if kind else 1 - odd, my_d, my_r, kind, c),
            send_sem=init_send.at[kind],
            recv_sem=chain_recv.at[my_d, 2 * my_r + kind],
            device_id=at(other if kind else mate, entry, c),
            device_id_type=MESH,
        )

    def slot_of(kind):
        return jnp.where(kind == 0, odd, 1 - odd)

    def chained(d, k):
        r, kind = k // 2, k % 2
        ref = place(slot_of(kind), d, r, kind, c)
        return pltpu.make_async_remote_copy(
            src_ref=ref,
            dst_ref=ref,
            send_sem=chain_send.at[d, k],
            recv_sem=chain_recv.at[d, k],
            device_id=at(f, jnp.where(d == 0, jnp.maximum(l - 1, 0), jnp.minimum(l + 1, line - 1)), c),
            device_id_type=MESH,
        )

    def sideways(d, k):
        r, kind = k // 2, k % 2
        return pltpu.make_async_remote_copy(
            src_ref=place(slot_of(kind), d, r, kind, c),
            dst_ref=place(1 - slot_of(kind), d, r, kind, c),
            send_sem=x_send.at[d, k],
            recv_sem=x_recv.at[d, k],
            device_id=at(jnp.where(kind == 0, ahead, behind), l, c),
            device_id_type=MESH,
        )

    def across(via, d, k):
        r, kind = k // 2, k % 2
        slot = slot_of(kind)
        ref = place(jnp.where(via == 0, slot, 1 - slot), d, r, kind, c)
        return pltpu.make_async_remote_copy(
            src_ref=ref,
            dst_ref=ref,
            send_sem=p_send.at[via, d, k],
            recv_sem=p_recv.at[via, d, k],
            device_id=at(f, l, 1 - c),
            device_id_type=MESH,
        )

    first(0).start()
    first(1).start()

    def steps_from_entry(d):
        return line - 1 - l if d == 0 else l

    @pl.loop(0, chunks + HOP * (line - 1) + SIDE)
    def _(n):
        for d in (0, 1):
            k = n - HOP * steps_from_entry(d)

            @pl.when((k >= 0) & (k < chunks))
            def _():
                chained(d, k).wait_recv()

                @pl.when(steps_from_entry(d) < line - 1)
                def _():
                    chained(d, k).start()

                sideways(d, k).start()
                across(0, d, k).start()

        for d in (0, 1):
            kx = n - HOP * steps_from_entry(d) - SIDE

            @pl.when((kx >= 0) & (kx < chunks))
            def _():
                sideways(d, kx).wait_recv()
                across(1, d, kx).start()

    @pl.loop(0, chunks)
    def _(k):
        for d in (0, 1):
            for via in (0, 1):
                across(via, d, k).wait_recv()

    first(0).wait_send()
    first(1).wait_send()

    @pl.loop(0, chunks)
    def _(k):
        for d in (0, 1):
            @pl.when(steps_from_entry(d) < line - 1)
            def _():
                chained(d, k).wait_send()

            sideways(d, k).wait_send()
            for via in (0, 1):
                across(via, d, k).wait_send()


def gather(own, frames, line):
    chunks = line
    dma = pltpu.SemaphoreType.DMA
    return pl.pallas_call(
        functools.partial(gather_kernel, frames, line),
        out_shape=jax.ShapeDtypeStruct((2, 2 * line, *own.shape), own.dtype),
        in_specs=[pl.BlockSpec(memory_space=pltpu.VMEM)],
        out_specs=pl.BlockSpec(memory_space=pltpu.VMEM),
        scratch_shapes=[
            dma((2,)),
            dma((2, chunks)),
            dma((2, chunks)),
            dma((2, 2, chunks)),
            dma((2, chunks)),
            dma((2, chunks)),
            dma((2, 2, chunks)),
        ],
        compiler_params=pltpu.CompilerParams(collective_id=0, has_side_effects=True),
        name="gather",
    )(own)


def pooling(out_rows, out_breadth):
    shape = (out_rows * out_breadth, 4 * out_rows * out_breadth)
    i = lax.broadcasted_iota(jnp.int32, shape, 0)
    q = lax.broadcasted_iota(jnp.int32, shape, 1)
    breadth = 2 * out_breadth
    row, column = q // breadth, q % breadth
    same = (row // 2 == i // out_breadth) & (column // 2 == i % out_breadth)
    return jnp.where(same, 0.25, 0.0).astype(jnp.bfloat16)


NT = (((1,), (1,)), ((), ()))


def dot(a, b):
    return jnp.dot(a, b, preferred_element_type=jnp.float32)


def dot_nt(a, b):
    return lax.dot_general(a, b, NT, preferred_element_type=jnp.float32)


def pyramid_kernel(frames, breadth, own, t, *rest):
    outs, (high1, low1, high2, low2) = rest[:8], rest[8:]
    f = lax.axis_index("frame")
    pixels = own.shape[0]
    rows = pixels // breadth
    targets = t.shape[1]
    factor = 1.0 / math.sqrt(own.shape[1])

    def put(ref, start, values):
        size = values.shape[1]
        for row in range(rows):
            ref[0, row, :, start:start + size] = values[row * breadth:(row + 1) * breadth]

    pool1 = pooling(1, breadth // 2)
    pool2 = pooling(2, breadth // 4)
    pool3 = pooling(4, breadth // 8)
    small = pool1.shape[0]

    def split(values):
        high = values.astype(jnp.bfloat16)
        return high, (values - high.astype(jnp.float32)).astype(jnp.bfloat16)

    for slot in (0, 1):
        valid = jnp.where(f < frames - 1, 1, 0) if slot == 0 else jnp.where(f > 0, 1, 0)
        scale = valid.astype(jnp.float32) * factor
        full, half, quarter, eighth = outs[4 * slot:4 * slot + 4]
        tile = 4 * pixels
        for start in range(0, targets, tile):
            scores = dot_nt(own[...], t[slot, start:start + tile])
            put(full, start, (scores * scale).astype(jnp.bfloat16))
        for u in range(targets // pixels):
            values = dot(pool1, t[slot, u * pixels:(u + 1) * pixels])
            high1[slot, u * small:(u + 1) * small], low1[slot, u * small:(u + 1) * small] = split(values)
        for u in range(targets // 4 // pixels):
            at = slice(u * pixels, (u + 1) * pixels)
            values = dot(pool2, high1[slot, at]) + dot(pool2, low1[slot, at])
            high2[slot, u * small:(u + 1) * small], low2[slot, u * small:(u + 1) * small] = split(values)
        high3, low3 = split(dot(pool3, high2[slot]) + dot(pool3, low2[slot]))
        for ref, high, low in ((half, high1[slot], low1[slot]), (quarter, high2[slot], low2[slot])):
            scores = dot_nt(own[...], high) + dot_nt(own[...], low)
            put(ref, 0, (scores * scale).astype(jnp.bfloat16))
        for row in range(rows):
            mine = own[row * breadth:(row + 1) * breadth]
            scores = dot_nt(high3, mine) + dot_nt(low3, mine)
            eighth[0, row] = (scores * scale).astype(jnp.bfloat16)


def pyramids(own, t, frames, rows, breadth):
    targets = t.shape[1]
    depths = [jax.ShapeDtypeStruct((1, rows, breadth, targets // 4**k), jnp.bfloat16) for k in range(3)]
    depths.append(jax.ShapeDtypeStruct((1, rows, targets // 64, breadth), jnp.bfloat16))
    scratch = [pltpu.VMEM((2, targets // 4**k, own.shape[1]), jnp.bfloat16) for k in (1, 1, 2, 2)]
    return pl.pallas_call(
        functools.partial(pyramid_kernel, frames, breadth),
        out_shape=depths * 2,
        in_specs=[pl.BlockSpec(memory_space=pltpu.VMEM)] * 2,
        out_specs=[pl.BlockSpec(memory_space=pltpu.VMEM)] * 8,
        scratch_shapes=scratch,
        name="pyramids",
    )(own, t)


def solution(mesh):
    frames = mesh.shape["frame"]
    line = mesh.shape["pix"] // 2

    def per_device(features):
        _, rows, breadth, channels = features.shape
        own = features.reshape(rows * breadth, channels)
        t = gather(own, frames, line)
        t = t.reshape(2, -1, channels)
        outs = list(pyramids(own, t, frames, rows, breadth))
        for k in (3, 7):
            outs[k] = outs[k].swapaxes(2, 3)
        return tuple(outs)

    spec = P(("clip", "frame"), "pix", None, None)
    return jax.shard_map(per_device, mesh=mesh, in_specs=(spec,), out_specs=(spec,) * 8, check_vma=False)
```

time: 161 us -> 71.5 us (0.44)
  blocking collectives: 86.1 us -> 0 us
  Pallas kernels: 0 us -> 70.6 us
  local copies, waits for them, and re-layouts: 21.5 us -> 0 us
  starting transfers between devices: 17.6 us -> 0 us
  waiting for transfers between devices: 16.3 us -> 0 us
  other arithmetic: 12.9 us -> 0 us
  matrix products: 4.15 us -> 0 us
    all_to_all x2 -> x0, blocking collectives: 86.1 us -> none  [sent_to_all(): lax.all_to_all(jnp.broadcast_to(array[None], (devices, *array.shape)), ax...]
    pallas_call x0 -> x2, Pallas kernels: none -> 70.6 us  [the longest x1 64.8 us: gather(): pl.pallas_call(functools.partial(gather_kernel, frames, line), out_shape=...]
    ppermute x2 -> x0, starting transfers between devices: 17.6 us -> none  [from_behind(): lax.ppermute(value, axis, [(source, source + steps) for source in range(l...]
    ppermute x2 -> x0, waiting for transfers between devices: 16.3 us -> none  [from_behind(): lax.ppermute(value, axis, [(source, source + steps) for source in range(l...]
    reduce_sum x6 -> x0, other arithmetic: 9.43 us -> none  [halved(): current.reshape(count, height // 2, 2, breadth // 2, 2).mean(axis=(2, 4))]
    another operation x2 -> x0, local copies, waits for them, and re-layouts: 7.65 us -> none  [halved(): current.reshape(count, height // 2, 2, breadth // 2, 2).mean(axis=(2, 4))]
    unnamed x10 -> x0, local copies, waits for them, and re-layouts: 5.38 us -> none
    mul x2 -> x0, local copies, waits for them, and re-layouts: 4.62 us -> none  [against(): return product * factor]
  transfers between devices with their start and end apart: 2 -> 0, of which waited for: 2 -> 0; matrix products, arithmetic and copies ran while one was open for 0% -> 0% of each run, Pallas kernels for 0% -> 0%
where the time goes in v1:
time: 71.5 us; the launch traced here: 71.3 us
  Pallas kernels  70.6 us (99%)
    pallas_call x1, Pallas kernels, gather(): pl.pallas_call(functools.partial(gather_kernel, frames, line), out_shape=...  64.8 us
    pallas_call x1, Pallas kernels, pyramids(): pl.pallas_call(functools.partial(pyramid_kernel, frames, breadth), out_sh...  5.84 us

profile of v1, /device:TPU:1, one launch (start us, length us, event | category | flops | bytes accessed | tf_op | source)
XLA Modules:
  0.0 71.3 jit_solution(3017485600873282067)
XLA Ops:
  0.6 64.8 %gather.1 = bf16[2,16,192,256]{3,2,1,0:T(8,128)(2,1)} custom-call(bf16[192,256]{1,0:T(8,128)(2,1)} %bitcast.5), custom_call_target="tpu_custom_call" | custom-call | tf_op jit(solution)/shard_map/gather/pallas_call | solution.py:177
  65.4 5.8 %pyramids.1 = (bf16[1,2,96,3072]{3,2,1,0:T(8,128)(2,1)}, bf16[1,2,96,768]{3,2,1,0:T(8,128)(2,1)}, bf16[1,2,96,192]{3,2,1,0:T(8,128)(2,1)}, bf16[1,2,48,96]{3,2,1...) custom-call(bf16[192,256]{1,0:T(8,128)(2,1)} %bitcast.6, ...), custom_call_target="tpu_custom_call" | custom-call | tf_op jit(solution)/shard_map/pyramids/pallas_call | solution.py:269

commit v2 on v1

--- a/solution.py
+++ b/solution.py
@@ -9,14 +9,19 @@
 from jax.sharding import PartitionSpec as P
 
 MESH = pl.DeviceIdType.MESH
-HOP = 2
-SIDE = 2
-
-
-def gather_kernel(frames, line, own, t, init_send, chain_send, x_send, p_send, chain_recv, x_recv, p_recv):
+SUB = 1
+SIDE = 8
+SWAP = 1
+EARLY = 1
+UNROLL = True
+MID = 2
+
+
+def gather_kernel(frames, line, own, t, init_send, on_send, back_send, x_send, p_send, chain_recv, x_recv, p_recv):
     half = own.shape[0] // 2
+    piece = half // SUB
     reach = line // 2
-    chunks = 2 * reach
+    chunks = 4 * SUB * reach
     f = lax.axis_index("frame")
     p = lax.axis_index("pix")
     l = p // 2
@@ -27,167 +32,190 @@
     other = (f - sign + frames) % frames
     ahead = (f + 2 * sign + frames) % frames
     behind = (f - 2 * sign + frames) % frames
+    d = (c + SWAP) % 2
+    u = jnp.where(d == 0, line - 1 - l, l)
+    my_d = jnp.where(l < reach, 0, 1)
+    my_r = jnp.where(l < reach, l, line - 1 - l)
+
+    def chip(d, steps):
+        return jnp.where(d == 0, line - 1 - steps, steps)
 
     def at(frame, chip, core):
         return {"frame": frame, "pix": 2 * chip + core}
 
+    def entry(r):
+        return jnp.where(r >= reach - EARLY, 0, MID)
+
     barrier = pltpu.get_barrier_semaphore()
 
     def greet(frame, chip, core):
         pl.semaphore_signal(barrier, inc=1, device_id=at(frame, chip, core), device_id_type=MESH)
+
+    for r in range(reach):
+        @pl.when(u == entry(r))
+        def _():
+            for core in (0, 1):
+                source = jnp.where(d == 0, r, line - 1 - r)
+                greet(mate, source, core)
+                greet(other, source, core)
 
     greet(f, l, 1 - c)
     greet(ahead, l, c)
     greet(behind, l, c)
 
-    @pl.when(l < line - 1)
+    @pl.when(u > 0)
     def _():
-        greet(f, l + 1, c)
-
-    @pl.when(l > 0)
+        greet(f, chip(d, u - 1), c)
+
+    @pl.when(u < MID)
     def _():
-        greet(f, l - 1, c)
-
-    @pl.when(l == line - 1)
-    def _():
-        for r in range(reach):
-            greet(mate, r, c)
-            greet(other, r, c)
-
-    @pl.when(l == 0)
-    def _():
-        for r in range(reach):
-            greet(mate, line - 1 - r, c)
-            greet(other, line - 1 - r, c)
-
-    inner = jnp.where((l > 0) & (l < line - 1), 1, 0)
-    pl.semaphore_wait(barrier, 6 + inner)
-
-    def place(slot, d, r, kind, core):
+        greet(f, chip(d, u + 1), c)
+
+    onward = jnp.where(u < line - 1, 1, 0)
+    backward = jnp.where((u >= 1) & (u <= MID), 1, 0)
+    pl.semaphore_wait(barrier, 5 + onward + backward)
+
+    def number(r, core, kind, sub):
+        return (((reach - 1 - r) * SUB + sub) * 2 + core) * 2 + kind
+
+    def fields(k):
+        return reach - 1 - k // (4 * SUB), k // 2 % 2, k % 2, k // 4 % SUB
+
+    def rows(kind, sub):
+        return pl.ds(pl.multiple_of(kind * half + sub * piece, piece), piece)
+
+    def slot_of(kind):
+        return jnp.where(kind == 0, odd, 1 - odd)
+
+    def place(slot, k):
+        r, core, kind, sub = fields(k)
         source = jnp.where(d == 0, r, line - 1 - r)
-        return t.at[slot, 2 * source + core, pl.ds(pl.multiple_of(kind * half, half), half)]
-
-    my_d = jnp.where(l < reach, 0, 1)
-    my_r = jnp.where(l < reach, l, line - 1 - l)
-    entry = jnp.where(l < reach, line - 1, 0)
-
-    def first(kind):
+        return t.at[slot, 2 * source + core, rows(kind, sub)]
+
+    def first(kind, sub):
+        k = number(my_r, c, kind, sub)
         return pltpu.make_async_remote_copy(
-            src_ref=own.at[pl.ds(kind * half, half)],
-            dst_ref=place(odd if kind else 1 - odd, my_d, my_r, kind, c),
-            send_sem=init_send.at[kind],
-            recv_sem=chain_recv.at[my_d, 2 * my_r + kind],
-            device_id=at(other if kind else mate, entry, c),
+            src_ref=own.at[rows(kind, sub)],
+            dst_ref=t.at[odd if kind else 1 - odd, p, rows(kind, sub)],
+            send_sem=init_send.at[kind, sub],
+            recv_sem=chain_recv.at[k],
+            device_id=at(other if kind else mate, chip(my_d, entry(my_r)), (my_d + SWAP) % 2),
             device_id_type=MESH,
         )
 
-    def slot_of(kind):
-        return jnp.where(kind == 0, odd, 1 - odd)
-
-    def chained(d, k):
-        r, kind = k // 2, k % 2
-        ref = place(slot_of(kind), d, r, kind, c)
+    def chained(k, step):
+        ref = place(slot_of(k % 2), k)
         return pltpu.make_async_remote_copy(
             src_ref=ref,
             dst_ref=ref,
-            send_sem=chain_send.at[d, k],
-            recv_sem=chain_recv.at[d, k],
-            device_id=at(f, jnp.where(d == 0, jnp.maximum(l - 1, 0), jnp.minimum(l + 1, line - 1)), c),
+            send_sem=(on_send if step > 0 else back_send).at[k],
+            recv_sem=chain_recv.at[k],
+            device_id=at(f, chip(d, jnp.clip(u + step, 0, line - 1)), c),
             device_id_type=MESH,
         )
 
-    def sideways(d, k):
-        r, kind = k // 2, k % 2
+    def sideways(k):
+        kind = k % 2
         return pltpu.make_async_remote_copy(
-            src_ref=place(slot_of(kind), d, r, kind, c),
-            dst_ref=place(1 - slot_of(kind), d, r, kind, c),
-            send_sem=x_send.at[d, k],
-            recv_sem=x_recv.at[d, k],
+            src_ref=place(slot_of(kind), k),
+            dst_ref=place(1 - slot_of(kind), k),
+            send_sem=x_send.at[k],
+            recv_sem=x_recv.at[k],
             device_id=at(jnp.where(kind == 0, ahead, behind), l, c),
             device_id_type=MESH,
         )
 
-    def across(via, d, k):
-        r, kind = k // 2, k % 2
-        slot = slot_of(kind)
-        ref = place(jnp.where(via == 0, slot, 1 - slot), d, r, kind, c)
+    def across(via, k, mine=True):
+        kind = k % 2
+        slot = slot_of(kind) if via == 0 else 1 - slot_of(kind)
+        r, core, kind, sub = fields(k)
+        low = jnp.where((d == 0) == mine, r, line - 1 - r)
+        ref = t.at[slot, 2 * low + core, rows(kind, sub)]
         return pltpu.make_async_remote_copy(
             src_ref=ref,
             dst_ref=ref,
-            send_sem=p_send.at[via, d, k],
-            recv_sem=p_recv.at[via, d, k],
+            send_sem=p_send.at[via, k],
+            recv_sem=p_recv.at[via, k],
             device_id=at(f, l, 1 - c),
             device_id_type=MESH,
         )
 
-    first(0).start()
-    first(1).start()
-
-    def steps_from_entry(d):
-        return line - 1 - l if d == 0 else l
-
-    @pl.loop(0, chunks + HOP * (line - 1) + SIDE)
-    def _(n):
-        for d in (0, 1):
-            k = n - HOP * steps_from_entry(d)
-
-            @pl.when((k >= 0) & (k < chunks))
-            def _():
-                chained(d, k).wait_recv()
-
-                @pl.when(steps_from_entry(d) < line - 1)
-                def _():
-                    chained(d, k).start()
-
-                sideways(d, k).start()
-                across(0, d, k).start()
-
-        for d in (0, 1):
-            kx = n - HOP * steps_from_entry(d) - SIDE
-
-            @pl.when((kx >= 0) & (kx < chunks))
-            def _():
-                sideways(d, kx).wait_recv()
-                across(1, d, kx).start()
-
-    @pl.loop(0, chunks)
-    def _(k):
-        for d in (0, 1):
-            for via in (0, 1):
-                across(via, d, k).wait_recv()
-
-    first(0).wait_send()
-    first(1).wait_send()
-
-    @pl.loop(0, chunks)
-    def _(k):
-        for d in (0, 1):
-            @pl.when(steps_from_entry(d) < line - 1)
-            def _():
-                chained(d, k).wait_send()
-
-            sideways(d, k).wait_send()
-            for via in (0, 1):
-                across(via, d, k).wait_send()
+    for sub in range(SUB):
+        for kind in (0, 1):
+            first(kind, sub).start()
+
+    def goes_on(k):
+        return (u >= entry(fields(k)[0])) & (u < line - 1)
+
+    def goes_back(k):
+        return (u <= entry(fields(k)[0])) & (u > 0)
+
+    def each(count, body):
+        if UNROLL:
+            for n in range(count):
+                body(n)
+        else:
+            pl.loop(0, count)(body)
+
+    def when(condition, body):
+        if isinstance(condition, bool):
+            if condition:
+                body()
+        else:
+            pl.when(condition)(body)
+
+    turn = jnp.where(u >= MID, 4 * SUB * EARLY, 0) if MID > 0 else 0
+
+    def step(n):
+        def arrived():
+            k = (n + turn) % chunks
+            chained(k, 1).wait_recv()
+            pl.when(goes_on(k))(lambda: chained(k, 1).start())
+            if MID > 0:
+                pl.when(goes_back(k))(lambda: chained(k, -1).start())
+            sideways(k).start()
+            across(0, k).start()
+
+        def came_over():
+            k = (n - SIDE + turn) % chunks
+            sideways(k).wait_recv()
+            across(1, k).start()
+
+        when(n < chunks, arrived)
+        when(n >= SIDE, came_over)
+
+    each(chunks + SIDE, step)
+
+    def last(k):
+        for via in (0, 1):
+            across(via, k, False).wait_recv()
+
+    each(chunks, last)
+
+    for sub in range(SUB):
+        for kind in (0, 1):
+            first(kind, sub).wait_send()
+
+    def sent(k):
+        pl.when(goes_on(k))(lambda: chained(k, 1).wait_send())
+        if MID > 0:
+            pl.when(goes_back(k))(lambda: chained(k, -1).wait_send())
+        sideways(k).wait_send()
+        for via in (0, 1):
+            across(via, k).wait_send()
+
+    each(chunks, sent)
 
 
 def gather(own, frames, line):
-    chunks = line
+    chunks = 2 * SUB * line
     dma = pltpu.SemaphoreType.DMA
     return pl.pallas_call(
         functools.partial(gather_kernel, frames, line),
-        out_shape=jax.ShapeDtypeStruct((2, 2 * line, *own.shape), own.dtype),
+        out_shape=pltpu.VMEM((2, 2 * line, *own.shape), own.dtype),
         in_specs=[pl.BlockSpec(memory_space=pltpu.VMEM)],
         out_specs=pl.BlockSpec(memory_space=pltpu.VMEM),
-        scratch_shapes=[
-            dma((2,)),
-            dma((2, chunks)),
-            dma((2, chunks)),
-            dma((2, 2, chunks)),
-            dma((2, chunks)),
-            dma((2, chunks)),
-            dma((2, 2, chunks)),
-        ],
+        scratch_shapes=[dma((2, SUB))] + [dma((chunks,))] * 3 + [dma((2, chunks))] + [dma((chunks,))] * 2 + [dma((2, chunks))],
         compiler_params=pltpu.CompilerParams(collective_id=0, has_side_effects=True),
         name="gather",
     )(own)
@@ -272,6 +300,7 @@
         in_specs=[pl.BlockSpec(memory_space=pltpu.VMEM)] * 2,
         out_specs=[pl.BlockSpec(memory_space=pltpu.VMEM)] * 8,
         scratch_shapes=scratch,
+        compiler_params=pltpu.CompilerParams(vmem_limit_bytes=32 * 2**20),
         name="pyramids",
     )(own, t)
 

time: 71.5 us -> 52.4 us (0.73)
  Pallas kernels: 70.6 us -> 51.5 us
    pallas_call x1, Pallas kernels: 64.8 us -> 47.5 us  [gather(): pl.pallas_call(functools.partial(gather_kernel, frames, line), out_shape=...]
    pallas_call x1, Pallas kernels: 5.84 us -> 3.93 us  [pyramids(): pl.pallas_call(functools.partial(pyramid_kernel, frames, breadth), out_sh...]
where the time goes in v2:
time: 52.4 us; the launch traced here: 52.1 us
  Pallas kernels  51.5 us (98%)
  between operations  0.66 us (1%)
    pallas_call x1, Pallas kernels, gather(): pl.pallas_call(functools.partial(gather_kernel, frames, line), out_shape=...  47.5 us
    pallas_call x1, Pallas kernels, pyramids(): pl.pallas_call(functools.partial(pyramid_kernel, frames, breadth), out_sh...  3.93 us

profile of v2, /device:TPU:1, one launch (start us, length us, event | category | flops | bytes accessed | tf_op | source)
XLA Modules:
  0.0 52.1 jit_solution(15711762801157815081)
XLA Ops:
  0.6 0.0 copy-start
  0.6 47.5 %gather.1 = bf16[2,16,192,256]{3,2,1,0:T(8,128)(2,1)S(1)} custom-call(bf16[192,256]{1,0:T(8,128)(2,1)} %bitcast.5), custom_call_target="tpu_custom_call" | custom-call | tf_op jit(solution)/shard_map/gather/pallas_call | solution.py:213
  48.2 0.0 copy-done
  48.2 3.9 %pyramids.1 = (bf16[1,2,96,3072]{3,2,1,0:T(8,128)(2,1)}, bf16[1,2,96,768]{3,2,1,0:T(8,128)(2,1)}, bf16[1,2,96,192]{3,2,1,0:T(8,128)(2,1)}, bf16[1,2,48,96]{3,2,1...) custom-call(bf16[192,256]{1,0:T(8,128)(2,1)S(1)} %bitcast.6, ...), custom_call_target="tpu_custom_call" | custom-call | tf_op jit(solution)/shard_map/pyramids/pallas_call | solution.py:297
Async XLA Ops:
  0.6 47.5 %copy-start = (bf16[1,2,96,256]{3,2,1,0:T(8,128)(2,1)S(1)}, bf16[1,2,96,256]{3,2,1,0:T(8,128)(2,1)}, u32[]{:S(2)}) copy-start(bf16[1,2,96,256]{3,2,1,0:T(8,128)(2,1)} %param.1) | copy-start | bytes 294916

commit v3 on v2

--- a/solution.py
+++ b/solution.py
@@ -12,9 +12,7 @@
 SUB = 1
 SIDE = 8
 SWAP = 1
-EARLY = 1
-UNROLL = True
-MID = 2
+WAYS = ((3, 1), (2, 2))
 
 
 def gather_kernel(frames, line, own, t, init_send, on_send, back_send, x_send, p_send, chain_recv, x_recv, p_recv):
@@ -43,17 +41,26 @@
     def at(frame, chip, core):
         return {"frame": frame, "pix": 2 * chip + core}
 
-    def entry(r):
-        return jnp.where(r >= reach - EARLY, 0, MID)
+    def way_in(parity, chain):
+        return jnp.where(
+            parity == 0,
+            jnp.where(chain == 0, WAYS[0][0], WAYS[0][1]),
+            jnp.where(chain == 0, WAYS[1][0], WAYS[1][1]),
+        )
+
+    here = way_in(odd, d)
+    there = way_in(1 - odd, my_d)
+    goes_on = (u >= here) & (u < line - 1)
+    goes_back = (u <= here) & (u > 0)
 
     barrier = pltpu.get_barrier_semaphore()
 
     def greet(frame, chip, core):
         pl.semaphore_signal(barrier, inc=1, device_id=at(frame, chip, core), device_id_type=MESH)
 
-    for r in range(reach):
-        @pl.when(u == entry(r))
-        def _():
+    @pl.when(u == here)
+    def _():
+        for r in range(reach):
             for core in (0, 1):
                 source = jnp.where(d == 0, r, line - 1 - r)
                 greet(mate, source, core)
@@ -67,13 +74,12 @@
     def _():
         greet(f, chip(d, u - 1), c)
 
-    @pl.when(u < MID)
+    @pl.when(u < line - 1)
     def _():
         greet(f, chip(d, u + 1), c)
 
-    onward = jnp.where(u < line - 1, 1, 0)
-    backward = jnp.where((u >= 1) & (u <= MID), 1, 0)
-    pl.semaphore_wait(barrier, 5 + onward + backward)
+    inner = jnp.where((u > 0) & (u < line - 1), 1, 0)
+    pl.semaphore_wait(barrier, 6 + inner)
 
     def number(r, core, kind, sub):
         return (((reach - 1 - r) * SUB + sub) * 2 + core) * 2 + kind
@@ -93,13 +99,12 @@
         return t.at[slot, 2 * source + core, rows(kind, sub)]
 
     def first(kind, sub):
-        k = number(my_r, c, kind, sub)
         return pltpu.make_async_remote_copy(
             src_ref=own.at[rows(kind, sub)],
             dst_ref=t.at[odd if kind else 1 - odd, p, rows(kind, sub)],
             send_sem=init_send.at[kind, sub],
-            recv_sem=chain_recv.at[k],
-            device_id=at(other if kind else mate, chip(my_d, entry(my_r)), (my_d + SWAP) % 2),
+            recv_sem=chain_recv.at[number(my_r, c, kind, sub)],
+            device_id=at(other if kind else mate, chip(my_d, there), (my_d + SWAP) % 2),
             device_id_type=MESH,
         )
 
@@ -140,71 +145,40 @@
             device_id_type=MESH,
         )
 
-    for sub in range(SUB):
-        for kind in (0, 1):
-            first(kind, sub).start()
-
-    def goes_on(k):
-        return (u >= entry(fields(k)[0])) & (u < line - 1)
-
-    def goes_back(k):
-        return (u <= entry(fields(k)[0])) & (u > 0)
-
-    def each(count, body):
-        if UNROLL:
-            for n in range(count):
-                body(n)
-        else:
-            pl.loop(0, count)(body)
-
-    def when(condition, body):
-        if isinstance(condition, bool):
-            if condition:
-                body()
-        else:
-            pl.when(condition)(body)
-
-    turn = jnp.where(u >= MID, 4 * SUB * EARLY, 0) if MID > 0 else 0
-
-    def step(n):
-        def arrived():
-            k = (n + turn) % chunks
-            chained(k, 1).wait_recv()
-            pl.when(goes_on(k))(lambda: chained(k, 1).start())
-            if MID > 0:
-                pl.when(goes_back(k))(lambda: chained(k, -1).start())
-            sideways(k).start()
-            across(0, k).start()
-
-        def came_over():
-            k = (n - SIDE + turn) % chunks
-            sideways(k).wait_recv()
-            across(1, k).start()
-
-        when(n < chunks, arrived)
-        when(n >= SIDE, came_over)
-
-    each(chunks + SIDE, step)
-
-    def last(k):
+    firsts = [first(kind, sub) for sub in range(SUB) for kind in (0, 1)]
+    for copy in firsts:
+        copy.start()
+
+    def arrived(k):
+        chained(k, 1).wait_recv()
+        pl.when(goes_on)(lambda: chained(k, 1).start())
+        pl.when(goes_back)(lambda: chained(k, -1).start())
+        sideways(k).start()
+        across(0, k).start()
+
+    def came_over(k):
+        sideways(k).wait_recv()
+        across(1, k).start()
+
+    for n in range(chunks + SIDE):
+        if n < chunks:
+            arrived(n)
+        if n >= SIDE:
+            came_over(n - SIDE)
+
+    for k in range(chunks):
         for via in (0, 1):
             across(via, k, False).wait_recv()
 
-    each(chunks, last)
-
-    for sub in range(SUB):
-        for kind in (0, 1):
-            first(kind, sub).wait_send()
-
-    def sent(k):
-        pl.when(goes_on(k))(lambda: chained(k, 1).wait_send())
-        if MID > 0:
-            pl.when(goes_back(k))(lambda: chained(k, -1).wait_send())
+    for copy in firsts:
+        copy.wait_send()
+
+    for k in range(chunks):
+        pl.when(goes_on)(lambda: chained(k, 1).wait_send())
+        pl.when(goes_back)(lambda: chained(k, -1).wait_send())
         sideways(k).wait_send()
         for via in (0, 1):
             across(via, k).wait_send()
-
-    each(chunks, sent)
 
 
 def gather(own, frames, line):
@@ -243,17 +217,24 @@
 
 
 def pyramid_kernel(frames, breadth, own, t, *rest):
-    outs, (high1, low1, high2, low2) = rest[:8], rest[8:]
+    outs, stage, (high1, low1, high2, low2, sem) = rest[:8], rest[8:16], rest[16:]
     f = lax.axis_index("frame")
     pixels = own.shape[0]
     rows = pixels // breadth
     targets = t.shape[1]
     factor = 1.0 / math.sqrt(own.shape[1])
-
-    def put(ref, start, values):
+    copies = []
+
+    def send(index, at):
+        copy = pltpu.make_async_copy(stage[index].at[at], outs[index].at[at], sem.at[len(copies)])
+        copy.start()
+        copies.append(copy)
+
+    def put(index, start, values):
         size = values.shape[1]
         for row in range(rows):
-            ref[0, row, :, start:start + size] = values[row * breadth:(row + 1) * breadth]
+            stage[index][0, row, :, start:start + size] = values[row * breadth:(row + 1) * breadth]
+        send(index, (slice(None), slice(None), slice(None), pl.ds(start, size)))
 
     pool1 = pooling(1, breadth // 2)
     pool2 = pooling(2, breadth // 4)
@@ -264,42 +245,51 @@
         high = values.astype(jnp.bfloat16)
         return high, (values - high.astype(jnp.float32)).astype(jnp.bfloat16)
 
+    scales = []
     for slot in (0, 1):
         valid = jnp.where(f < frames - 1, 1, 0) if slot == 0 else jnp.where(f > 0, 1, 0)
-        scale = valid.astype(jnp.float32) * factor
-        full, half, quarter, eighth = outs[4 * slot:4 * slot + 4]
-        tile = 4 * pixels
+        scales.append(valid.astype(jnp.float32) * factor)
+    tile = 4 * pixels
+    for slot in (0, 1):
         for start in range(0, targets, tile):
             scores = dot_nt(own[...], t[slot, start:start + tile])
-            put(full, start, (scores * scale).astype(jnp.bfloat16))
-        for u in range(targets // pixels):
-            values = dot(pool1, t[slot, u * pixels:(u + 1) * pixels])
-            high1[slot, u * small:(u + 1) * small], low1[slot, u * small:(u + 1) * small] = split(values)
-        for u in range(targets // 4 // pixels):
-            at = slice(u * pixels, (u + 1) * pixels)
+            put(4 * slot, start, (scores * scales[slot]).astype(jnp.bfloat16))
+    for slot in (0, 1):
+        for v in range(targets // pixels):
+            values = dot(pool1, t[slot, v * pixels:(v + 1) * pixels])
+            high1[slot, v * small:(v + 1) * small], low1[slot, v * small:(v + 1) * small] = split(values)
+        scores = dot_nt(own[...], high1[slot]) + dot_nt(own[...], low1[slot])
+        put(4 * slot + 1, 0, (scores * scales[slot]).astype(jnp.bfloat16))
+    for slot in (0, 1):
+        for v in range(targets // 4 // pixels):
+            at = slice(v * pixels, (v + 1) * pixels)
             values = dot(pool2, high1[slot, at]) + dot(pool2, low1[slot, at])
-            high2[slot, u * small:(u + 1) * small], low2[slot, u * small:(u + 1) * small] = split(values)
+            high2[slot, v * small:(v + 1) * small], low2[slot, v * small:(v + 1) * small] = split(values)
+        scores = dot_nt(own[...], high2[slot]) + dot_nt(own[...], low2[slot])
+        put(4 * slot + 2, 0, (scores * scales[slot]).astype(jnp.bfloat16))
         high3, low3 = split(dot(pool3, high2[slot]) + dot(pool3, low2[slot]))
-        for ref, high, low in ((half, high1[slot], low1[slot]), (quarter, high2[slot], low2[slot])):
-            scores = dot_nt(own[...], high) + dot_nt(own[...], low)
-            put(ref, 0, (scores * scale).astype(jnp.bfloat16))
         for row in range(rows):
             mine = own[row * breadth:(row + 1) * breadth]
             scores = dot_nt(high3, mine) + dot_nt(low3, mine)
-            eighth[0, row] = (scores * scale).astype(jnp.bfloat16)
+            stage[4 * slot + 3][0, row] = (scores * scales[slot]).astype(jnp.bfloat16)
+        send(4 * slot + 3, (slice(None),))
+    for copy in copies:
+        copy.wait()
 
 
 def pyramids(own, t, frames, rows, breadth):
     targets = t.shape[1]
-    depths = [jax.ShapeDtypeStruct((1, rows, breadth, targets // 4**k), jnp.bfloat16) for k in range(3)]
-    depths.append(jax.ShapeDtypeStruct((1, rows, targets // 64, breadth), jnp.bfloat16))
+    pixels = own.shape[0]
+    depths = [(1, rows, breadth, targets // 4**k) for k in range(3)] + [(1, rows, targets // 64, breadth)]
     scratch = [pltpu.VMEM((2, targets // 4**k, own.shape[1]), jnp.bfloat16) for k in (1, 1, 2, 2)]
     return pl.pallas_call(
         functools.partial(pyramid_kernel, frames, breadth),
-        out_shape=depths * 2,
+        out_shape=[jax.ShapeDtypeStruct(shape, jnp.bfloat16) for shape in depths * 2],
         in_specs=[pl.BlockSpec(memory_space=pltpu.VMEM)] * 2,
-        out_specs=[pl.BlockSpec(memory_space=pltpu.VMEM)] * 8,
-        scratch_shapes=scratch,
+        out_specs=[pl.BlockSpec(memory_space=pltpu.HBM)] * 8,
+        scratch_shapes=[pltpu.VMEM(shape, jnp.bfloat16) for shape in depths * 2]
+        + scratch
+        + [pltpu.SemaphoreType.DMA((2 * (targets // (4 * pixels) + 3),))],
         compiler_params=pltpu.CompilerParams(vmem_limit_bytes=32 * 2**20),
         name="pyramids",
     )(own, t)

time: 52.4 us -> 51.1 us (0.975)
  the two profiles are of different devices: /device:TPU:1 before, /device:TPU:505 now
where the time goes in v3:
time: 51.1 us; the launch traced here: 51 us
  Pallas kernels  50.3 us (98%)
  between operations  0.66 us (1%)
    pallas_call x1, Pallas kernels, gather(): pl.pallas_call(functools.partial(gather_kernel, frames, line), out_shape=...  46.5 us
    pallas_call x1, Pallas kernels, pyramids(): pl.pallas_call(functools.partial(pyramid_kernel, frames, breadth), out_sh...  3.85 us

profile of v3, /device:TPU:505, one launch (start us, length us, event | category | flops | bytes accessed | tf_op | source)
XLA Modules:
  0.0 51.0 jit_solution(3999149691367134771)
XLA Ops:
  0.6 0.0 copy-start
  0.6 46.5 %gather.1 = bf16[2,16,192,256]{3,2,1,0:T(8,128)(2,1)S(1)} custom-call(bf16[192,256]{1,0:T(8,128)(2,1)} %bitcast.5), custom_call_target="tpu_custom_call" | custom-call | tf_op jit(solution)/shard_map/gather/pallas_call | solution.py:187
  47.1 0.0 copy-done
  47.1 3.9 %pyramids.1 = (bf16[1,2,96,3072]{3,2,1,0:T(8,128)(2,1)}, bf16[1,2,96,768]{3,2,1,0:T(8,128)(2,1)}, bf16[1,2,96,192]{3,2,1,0:T(8,128)(2,1)}, bf16[1,2,48,96]{3,2,1...) custom-call(bf16[192,256]{1,0:T(8,128)(2,1)S(1)} %bitcast.6, ...), custom_call_target="tpu_custom_call" | custom-call | tf_op jit(solution)/shard_map/pyramids/pallas_call | solution.py:285
Async XLA Ops:
  0.6 46.5 %copy-start = (bf16[1,2,96,256]{3,2,1,0:T(8,128)(2,1)S(1)}, bf16[1,2,96,256]{3,2,1,0:T(8,128)(2,1)}, u32[]{:S(2)}) copy-start(bf16[1,2,96,256]{3,2,1,0:T(8,128)(2,1)} %param.1) | copy-start | bytes 294916

commit v4 on v3

--- a/solution.py
+++ b/solution.py
@@ -15,7 +15,39 @@
 WAYS = ((3, 1), (2, 2))
 
 
-def gather_kernel(frames, line, own, t, init_send, on_send, back_send, x_send, p_send, chain_recv, x_recv, p_recv):
+def pooling(out_rows, out_breadth):
+    shape = (out_rows * out_breadth, 4 * out_rows * out_breadth)
+    i = lax.broadcasted_iota(jnp.int32, shape, 0)
+    q = lax.broadcasted_iota(jnp.int32, shape, 1)
+    breadth = 2 * out_breadth
+    row, column = q // breadth, q % breadth
+    same = (row // 2 == i // out_breadth) & (column // 2 == i % out_breadth)
+    return jnp.where(same, 0.25, 0.0).astype(jnp.bfloat16)
+
+
+NT = (((1,), (1,)), ((), ()))
+
+
+def dot(a, b):
+    return jnp.dot(a, b, preferred_element_type=jnp.float32)
+
+
+def dot_nt(a, b):
+    return lax.dot_general(a, b, NT, preferred_element_type=jnp.float32)
+
+
+def split(values):
+    high = values.astype(jnp.bfloat16)
+    return high, (values - high.astype(jnp.float32)).astype(jnp.bfloat16)
+
+
+def scale_of(frames, slot, channels):
+    f = lax.axis_index("frame")
+    valid = jnp.where(f < frames - 1, 1, 0) if slot == 0 else jnp.where(f > 0, 1, 0)
+    return valid.astype(jnp.float32) * (1.0 / math.sqrt(channels))
+
+
+def gather_kernel(frames, line, breadth, own, scores0, high1, low1, t, init_send, on_send, back_send, x_send, p_send, chain_recv, x_recv, p_recv):
     half = own.shape[0] // 2
     piece = half // SUB
     reach = line // 2
@@ -160,15 +192,46 @@
         sideways(k).wait_recv()
         across(1, k).start()
 
+    pixels, channels = own.shape
+    pool1 = pooling(1, breadth // 2)
+    small = pool1.shape[0]
+
+    def use(group, mine):
+        r = reach - 1 - group
+        source = jnp.where((d == 0) == mine, r, line - 1 - r)
+        for slot in (0, 1):
+            targets = t[slot, pl.ds(2 * source, 2)].reshape(2 * pixels, channels)
+            scores = (dot_nt(own[...], targets) * scale_of(frames, slot, channels)).astype(jnp.bfloat16)
+            columns = pl.ds(pl.multiple_of(2 * pixels * source, 128), 2 * pixels)
+            for row in range(pixels // breadth):
+                scores0[slot, 0, row, :, columns] = scores[row * breadth:(row + 1) * breadth]
+            for core in (0, 1):
+                values = dot(pool1, targets[core * pixels:(core + 1) * pixels])
+                at = pl.ds(pl.multiple_of((2 * source + core) * small, small), small)
+                high1[slot, at], low1[slot, at] = split(values)
+
+    per_group = 4 * SUB
+
+    def use_across(group):
+        for k in range(per_group * group, per_group * (group + 1)):
+            for via in (0, 1):
+                across(via, k, False).wait_recv()
+        use(group, False)
+
     for n in range(chunks + SIDE):
         if n < chunks:
             arrived(n)
         if n >= SIDE:
             came_over(n - SIDE)
-
-    for k in range(chunks):
-        for via in (0, 1):
-            across(via, k, False).wait_recv()
+            if (n - SIDE) % per_group == per_group - 1:
+                group = (n - SIDE) // per_group
+                pl.when(u >= reach)(lambda: use_across(group))
+                use(group, True)
+
+    @pl.when(u < reach)
+    def _():
+        for group in range(reach):
+            use_across(group)
 
     for copy in firsts:
         copy.wait_send()
@@ -181,118 +244,83 @@
             across(via, k).wait_send()
 
 
-def gather(own, frames, line):
+def gather(own, frames, line, breadth):
+    pixels, channels = own.shape
+    targets = 2 * line * pixels
     chunks = 2 * SUB * line
     dma = pltpu.SemaphoreType.DMA
+    averages = pltpu.VMEM((2, targets // 4, channels), own.dtype)
     return pl.pallas_call(
-        functools.partial(gather_kernel, frames, line),
-        out_shape=pltpu.VMEM((2, 2 * line, *own.shape), own.dtype),
+        functools.partial(gather_kernel, frames, line, breadth),
+        out_shape=[pltpu.VMEM((2, 1, pixels // breadth, breadth, targets), own.dtype), averages, averages],
         in_specs=[pl.BlockSpec(memory_space=pltpu.VMEM)],
-        out_specs=pl.BlockSpec(memory_space=pltpu.VMEM),
-        scratch_shapes=[dma((2, SUB))] + [dma((chunks,))] * 3 + [dma((2, chunks))] + [dma((chunks,))] * 2 + [dma((2, chunks))],
-        compiler_params=pltpu.CompilerParams(collective_id=0, has_side_effects=True),
+        out_specs=[pl.BlockSpec(memory_space=pltpu.VMEM)] * 3,
+        scratch_shapes=[pltpu.VMEM((2, 2 * line, *own.shape), own.dtype)]
+        + [dma((2, SUB))] + [dma((chunks,))] * 3 + [dma((2, chunks))] + [dma((chunks,))] * 2 + [dma((2, chunks))],
+        compiler_params=pltpu.CompilerParams(collective_id=0, has_side_effects=True, vmem_limit_bytes=32 * 2**20),
         name="gather",
     )(own)
 
 
-def pooling(out_rows, out_breadth):
-    shape = (out_rows * out_breadth, 4 * out_rows * out_breadth)
-    i = lax.broadcasted_iota(jnp.int32, shape, 0)
-    q = lax.broadcasted_iota(jnp.int32, shape, 1)
-    breadth = 2 * out_breadth
-    row, column = q // breadth, q % breadth
-    same = (row // 2 == i // out_breadth) & (column // 2 == i % out_breadth)
-    return jnp.where(same, 0.25, 0.0).astype(jnp.bfloat16)
-
-
-NT = (((1,), (1,)), ((), ()))
-
-
-def dot(a, b):
-    return jnp.dot(a, b, preferred_element_type=jnp.float32)
-
-
-def dot_nt(a, b):
-    return lax.dot_general(a, b, NT, preferred_element_type=jnp.float32)
-
-
-def pyramid_kernel(frames, breadth, own, t, *rest):
-    outs, stage, (high1, low1, high2, low2, sem) = rest[:8], rest[8:16], rest[16:]
-    f = lax.axis_index("frame")
-    pixels = own.shape[0]
+def pyramid_kernel(frames, breadth, own, scores0, high1, low1, *rest):
+    outs, stage, (high2, low2, sem) = rest[:8], rest[8:14], rest[14:]
+    pixels, channels = own.shape
     rows = pixels // breadth
-    targets = t.shape[1]
-    factor = 1.0 / math.sqrt(own.shape[1])
     copies = []
 
-    def send(index, at):
-        copy = pltpu.make_async_copy(stage[index].at[at], outs[index].at[at], sem.at[len(copies)])
+    def send(source, target):
+        copy = pltpu.make_async_copy(source, target, sem.at[len(copies)])
         copy.start()
         copies.append(copy)
 
-    def put(index, start, values):
-        size = values.shape[1]
-        for row in range(rows):
-            stage[index][0, row, :, start:start + size] = values[row * breadth:(row + 1) * breadth]
-        send(index, (slice(None), slice(None), slice(None), pl.ds(start, size)))
-
-    pool1 = pooling(1, breadth // 2)
+    for slot in (0, 1):
+        send(scores0.at[slot], outs[4 * slot])
+
     pool2 = pooling(2, breadth // 4)
     pool3 = pooling(4, breadth // 8)
-    small = pool1.shape[0]
-
-    def split(values):
-        high = values.astype(jnp.bfloat16)
-        return high, (values - high.astype(jnp.float32)).astype(jnp.bfloat16)
-
-    scales = []
+    small = pool2.shape[0]
+
     for slot in (0, 1):
-        valid = jnp.where(f < frames - 1, 1, 0) if slot == 0 else jnp.where(f > 0, 1, 0)
-        scales.append(valid.astype(jnp.float32) * factor)
-    tile = 4 * pixels
-    for slot in (0, 1):
-        for start in range(0, targets, tile):
-            scores = dot_nt(own[...], t[slot, start:start + tile])
-            put(4 * slot, start, (scores * scales[slot]).astype(jnp.bfloat16))
-    for slot in (0, 1):
-        for v in range(targets // pixels):
-            values = dot(pool1, t[slot, v * pixels:(v + 1) * pixels])
-            high1[slot, v * small:(v + 1) * small], low1[slot, v * small:(v + 1) * small] = split(values)
-        scores = dot_nt(own[...], high1[slot]) + dot_nt(own[...], low1[slot])
-        put(4 * slot + 1, 0, (scores * scales[slot]).astype(jnp.bfloat16))
-    for slot in (0, 1):
-        for v in range(targets // 4 // pixels):
+        half, quarter, eighth = stage[3 * slot:3 * slot + 3]
+        scale = scale_of(frames, slot, channels)
+
+        def put(ref, out, high, low):
+            scores = dot_nt(own[...], high) + dot_nt(own[...], low)
+            scores = (scores * scale).astype(jnp.bfloat16)
+            for row in range(rows):
+                ref[0, row] = scores[row * breadth:(row + 1) * breadth]
+            send(ref, out)
+
+        put(half, outs[4 * slot + 1], high1[slot], low1[slot])
+        for v in range(high1.shape[1] // pixels):
             at = slice(v * pixels, (v + 1) * pixels)
             values = dot(pool2, high1[slot, at]) + dot(pool2, low1[slot, at])
             high2[slot, v * small:(v + 1) * small], low2[slot, v * small:(v + 1) * small] = split(values)
-        scores = dot_nt(own[...], high2[slot]) + dot_nt(own[...], low2[slot])
-        put(4 * slot + 2, 0, (scores * scales[slot]).astype(jnp.bfloat16))
+        put(quarter, outs[4 * slot + 2], high2[slot], low2[slot])
         high3, low3 = split(dot(pool3, high2[slot]) + dot(pool3, low2[slot]))
         for row in range(rows):
             mine = own[row * breadth:(row + 1) * breadth]
             scores = dot_nt(high3, mine) + dot_nt(low3, mine)
-            stage[4 * slot + 3][0, row] = (scores * scales[slot]).astype(jnp.bfloat16)
-        send(4 * slot + 3, (slice(None),))
+            eighth[0, row] = (scores * scale).astype(jnp.bfloat16)
+        send(eighth, outs[4 * slot + 3])
     for copy in copies:
         copy.wait()
 
 
-def pyramids(own, t, frames, rows, breadth):
-    targets = t.shape[1]
-    pixels = own.shape[0]
+def pyramids(own, scores0, high1, low1, frames):
+    _, _, rows, breadth, targets = scores0.shape
     depths = [(1, rows, breadth, targets // 4**k) for k in range(3)] + [(1, rows, targets // 64, breadth)]
-    scratch = [pltpu.VMEM((2, targets // 4**k, own.shape[1]), jnp.bfloat16) for k in (1, 1, 2, 2)]
     return pl.pallas_call(
         functools.partial(pyramid_kernel, frames, breadth),
         out_shape=[jax.ShapeDtypeStruct(shape, jnp.bfloat16) for shape in depths * 2],
-        in_specs=[pl.BlockSpec(memory_space=pltpu.VMEM)] * 2,
+        in_specs=[pl.BlockSpec(memory_space=pltpu.VMEM)] * 4,
         out_specs=[pl.BlockSpec(memory_space=pltpu.HBM)] * 8,
-        scratch_shapes=[pltpu.VMEM(shape, jnp.bfloat16) for shape in depths * 2]
-        + scratch
-        + [pltpu.SemaphoreType.DMA((2 * (targets // (4 * pixels) + 3),))],
+        scratch_shapes=[pltpu.VMEM(shape, jnp.bfloat16) for shape in depths[1:] * 2]
+        + [pltpu.VMEM((2, targets // 16, own.shape[1]), jnp.bfloat16)] * 2
+        + [pltpu.SemaphoreType.DMA((8,))],
         compiler_params=pltpu.CompilerParams(vmem_limit_bytes=32 * 2**20),
         name="pyramids",
-    )(own, t)
+    )(own, scores0, high1, low1)
 
 
 def solution(mesh):
@@ -302,9 +330,7 @@
     def per_device(features):
         _, rows, breadth, channels = features.shape
         own = features.reshape(rows * breadth, channels)
-        t = gather(own, frames, line)
-        t = t.reshape(2, -1, channels)
-        outs = list(pyramids(own, t, frames, rows, breadth))
+        outs = list(pyramids(own, *gather(own, frames, line, breadth), frames))
         for k in (3, 7):
             outs[k] = outs[k].swapaxes(2, 3)
         return tuple(outs)

time: 51.1 us -> 50.3 us (0.984)
  the two profiles are of different devices: /device:TPU:505 before, /device:TPU:1 now
where the time goes in v4:
time: 50.3 us; the launch traced here: 49.7 us
  Pallas kernels  48.2 us (96%)
  local copies, waits for them, and re-layouts  0.89 us (2%)
  between operations  0.65 us (1%)
    pallas_call x1, Pallas kernels, gather(): pl.pallas_call(functools.partial(gather_kernel, frames, line, breadth), o...  45.8 us
    pallas_call x1, Pallas kernels, pyramids(): pl.pallas_call(functools.partial(pyramid_kernel, frames, breadth), out_sh...  2.42 us

profile of v4, /device:TPU:1, one launch (start us, length us, event | category | flops | bytes accessed | tf_op | source)
XLA Modules:
  0.0 49.7 jit_solution(2726647783530536779)
XLA Ops:
  0.6 0.0 copy-start
  0.6 0.9 %copy-done = bf16[1,2,96,256]{3,2,1,0:T(8,128)(2,1)S(1)} copy-done((bf16[1,2,96,256]{3,2,1,0:T(8,128)(2,1)S(1)}, bf16[1,2,96,256]{3,2,1,0:T(8,128)(2,1)}, u32[]{:S(2)}) %copy-start) | copy-done | bytes 98328
  1.5 45.8 %gather.1 = (bf16[2,1,2,96,3072]{4,3,2,1,0:T(8,128)(2,1)S(1)}, bf16[2,768,256]{2,1,0:T(8,128)(2,1)S(1)}, bf16[2,768,256]{2,1,0:T(8,128)(2,1)S(1)}) custom-call(bf16[192,256]{1,0:T(8,128)(2,1)S(1)} %bitcast.3), custom_call_target="tpu_custom_call" | custom-call | tf_op jit(solution)/shard_map/gather/pallas_call | solution.py:253
  47.3 2.4 %pyramids.1 = (bf16[1,2,96,3072]{3,2,1,0:T(8,128)(2,1)}, bf16[1,2,96,768]{3,2,1,0:T(8,128)(2,1)}, bf16[1,2,96,192]{3,2,1,0:T(8,128)(2,1)}, bf16[1,2,48,96]{3,2,1...) custom-call(bf16[192,256]{1,0:T(8,128)(2,1)S(1)} %bitcast.4, ...), custom_call_target="tpu_custom_call" | custom-call | tf_op jit(solution)/shard_map/pyramids/pallas_call | solution.py:313
Async XLA Ops:
  0.6 0.9 %copy-start = (bf16[1,2,96,256]{3,2,1,0:T(8,128)(2,1)S(1)}, bf16[1,2,96,256]{3,2,1,0:T(8,128)(2,1)}, u32[]{:S(2)}) copy-start(bf16[1,2,96,256]{3,2,1,0:T(8,128)(2,1)} %param.1) | copy-start | bytes 294916

commit v5 on v4

--- a/solution.py
+++ b/solution.py
@@ -11,7 +11,6 @@
 MESH = pl.DeviceIdType.MESH
 SUB = 1
 SIDE = 8
-SWAP = 1
 WAYS = ((3, 1), (2, 2))
 
 
@@ -62,7 +61,7 @@
     other = (f - sign + frames) % frames
     ahead = (f + 2 * sign + frames) % frames
     behind = (f - 2 * sign + frames) % frames
-    d = (c + SWAP) % 2
+    d = (c + 1 - odd) % 2
     u = jnp.where(d == 0, line - 1 - l, l)
     my_d = jnp.where(l < reach, 0, 1)
     my_r = jnp.where(l < reach, l, line - 1 - l)
@@ -136,7 +135,7 @@
             dst_ref=t.at[odd if kind else 1 - odd, p, rows(kind, sub)],
             send_sem=init_send.at[kind, sub],
             recv_sem=chain_recv.at[number(my_r, c, kind, sub)],
-            device_id=at(other if kind else mate, chip(my_d, there), (my_d + SWAP) % 2),
+            device_id=at(other if kind else mate, chip(my_d, there), (my_d + odd) % 2),
             device_id_type=MESH,
         )
 

time: 50.3 us -> 50 us (level)
  no operation moved by 1% of the time
where the time goes in v5:
time: 50 us; the launch traced here: 49.8 us
  Pallas kernels  48.3 us (97%)
  local copies, waits for them, and re-layouts  0.89 us (2%)
  between operations  0.65 us (1%)
    pallas_call x1, Pallas kernels, gather(): pl.pallas_call(functools.partial(gather_kernel, frames, line, breadth), o...  45.9 us
    pallas_call x1, Pallas kernels, pyramids(): pl.pallas_call(functools.partial(pyramid_kernel, frames, breadth), out_sh...  2.42 us

profile of v5, /device:TPU:1, one launch (start us, length us, event | category | flops | bytes accessed | tf_op | source)
XLA Modules:
  0.0 49.8 jit_solution(13528196919741804642)
XLA Ops:
  0.6 0.0 copy-start
  0.6 0.9 %copy-done = bf16[1,2,96,256]{3,2,1,0:T(8,128)(2,1)S(1)} copy-done((bf16[1,2,96,256]{3,2,1,0:T(8,128)(2,1)S(1)}, bf16[1,2,96,256]{3,2,1,0:T(8,128)(2,1)}, u32[]{:S(2)}) %copy-start) | copy-done | bytes 98328
  1.5 45.9 %gather.1 = (bf16[2,1,2,96,3072]{4,3,2,1,0:T(8,128)(2,1)S(1)}, bf16[2,768,256]{2,1,0:T(8,128)(2,1)S(1)}, bf16[2,768,256]{2,1,0:T(8,128)(2,1)S(1)}) custom-call(bf16[192,256]{1,0:T(8,128)(2,1)S(1)} %bitcast.3), custom_call_target="tpu_custom_call" | custom-call | tf_op jit(solution)/shard_map/gather/pallas_call | solution.py:252
  47.4 2.4 %pyramids.1 = (bf16[1,2,96,3072]{3,2,1,0:T(8,128)(2,1)}, bf16[1,2,96,768]{3,2,1,0:T(8,128)(2,1)}, bf16[1,2,96,192]{3,2,1,0:T(8,128)(2,1)}, bf16[1,2,48,96]{3,2,1...) custom-call(bf16[192,256]{1,0:T(8,128)(2,1)S(1)} %bitcast.4, ...), custom_call_target="tpu_custom_call" | custom-call | tf_op jit(solution)/shard_map/pyramids/pallas_call | solution.py:312
Async XLA Ops:
  0.6 0.9 %copy-start = (bf16[1,2,96,256]{3,2,1,0:T(8,128)(2,1)S(1)}, bf16[1,2,96,256]{3,2,1,0:T(8,128)(2,1)}, u32[]{:S(2)}) copy-start(bf16[1,2,96,256]{3,2,1,0:T(8,128)(2,1)} %param.1) | copy-start | bytes 294916
